TPU v7x, 32 devices: a whole 2x2x4 slice. The times are simulated.
32 devices in a mesh: groups: 2 (over y), epoch: 4 (over z), space: 2 (over x), sub: 2 (over core).
Axes of the slice: x: 2, y: 2, z: 4, core: 2. Of those that a mesh axis runs over, the one named last changes fastest.
Arguments:
- slc: bfloat16 [2, 64, 128, 1024], P(None, ('groups', 'epoch'), 'space', 'sub'), parts along dimension 1, may hold values from -8 to 8
- offsets: int32 [64, 4], P(('groups', 'epoch')), parts along dimension 0, may hold values from 1 to 8, as said below
- weights: float32 [64, 4], P(('groups', 'epoch')), parts along dimension 0, may hold values from 0.3 to 3
- estimate: float32 [64, 32, 1024], P(('groups', 'epoch'), 'space', 'sub'), parts along dimension 0, may hold values from -2 to 2
- direction: float32 [64, 32, 1024], P(('groups', 'epoch'), 'space', 'sub'), parts along dimension 0, may hold values from -2 to 2
- prev_mean: float32 [1], replicated, may hold values from 0.05 to 0.5
Outputs:
- new_estimate: float32 [64, 32, 1024], P(('groups', 'epoch'), 'space', 'sub'), parts along dimension 0
- new_direction: float32 [64, 32, 1024], P(('groups', 'epoch'), 'space', 'sub'), parts along dimension 0
There are 2 independent parts, one for each index of `groups`. A program takes and returns all parts, laid end to end along the dimension named above; an argument that names none is the same for every part. Nothing has to cross between parts.
Inputs may be any that keep to these rules, and one draw needn't show every extreme that they name: `offsets`: each row holds 4 different distances; partners wrap past the last epoch to the first.
All inputs are finite; a program needn't handle non-finite values.
Results may differ from a plain program's by a relative error of at most 0.0003.
Values may be sent and summed in bfloat16 or wider, within the bound.
A program may use at most 64 MiB of HBM per device.

v0:
```python
import jax
import jax.numpy as jnp
from jax import lax
from jax.sharding import PartitionSpec as P

SLOTS = 4
OFFS = 8
LOOK = 4
RADIUS = 3
EPSILON = 1e-06


def passed_along(x, axis, by):
    size = lax.axis_size(axis)
    return lax.ppermute(x, axis, [(i, (i + by) % size) for i in range(size)])


def extended_2(block, sides, width):
    for axis, dim in sides:
        count = lax.axis_size(axis)
        forward = [(i, i + 1) for i in range(count - 1)]
        backward = [(target, source) for source, target in forward]
        low = lax.ppermute(
            lax.slice_in_dim(block, block.shape[dim] - width, None, axis=dim), axis, forward
        )
        high = lax.ppermute(lax.slice_in_dim(block, 0, width, axis=dim), axis, backward)
        block = jnp.concatenate([low, block, high], axis=dim)
    return block


def looked_sum(field):
    shape = field.shape
    return jnp.sum(field.reshape(shape[:-2] + (shape[-2] // LOOK, LOOK, shape[-1])), axis=-2)


def window_sum(padded, axis):
    length = padded.shape[axis] - 2 * RADIUS
    total = lax.slice_in_dim(padded, 0, length, axis=axis)
    for shift_at in range(1, 2 * RADIUS + 1):
        total = total + lax.slice_in_dim(padded, shift_at, shift_at + length, axis=axis)
    return total


def on_device(slc, offsets, weights, estimate, direction, prev_mean):
    epochs_here = slc.shape[1]
    look_rows = slc.shape[2] // LOOK
    col_count = slc.shape[3]
    ahead = passed_along(slc, "epoch", -1)
    extended = jnp.concatenate([slc, ahead], axis=1)
    numbers = jnp.arange(epochs_here, dtype=jnp.int32)
    partner = numbers[:, None] + offsets
    own_real = slc[0].astype(jnp.float32)
    own_imag = slc[1].astype(jnp.float32)
    ext_real = extended[0].astype(jnp.float32)
    ext_imag = extended[1].astype(jnp.float32)
    powers = looked_sum(ext_real * ext_real + ext_imag * ext_imag)
    pieces = []
    for slot_index in range(SLOTS):
        mate_real = jnp.take(ext_real, partner[:, slot_index], axis=0)
        mate_imag = jnp.take(ext_imag, partner[:, slot_index], axis=0)
        pieces.append(looked_sum(own_real * mate_real + own_imag * mate_imag))
        pieces.append(looked_sum(own_imag * mate_real - own_real * mate_imag))
    pair_count = epochs_here * 2 * SLOTS
    stacked = jnp.concatenate(
        [jnp.stack(pieces, axis=1).reshape(pair_count, look_rows, col_count), powers], axis=0
    )
    padded = extended_2(stacked, (("space", 1), ("sub", 2)), RADIUS)
    boxed = window_sum(window_sum(padded, 1), 2)
    pair_boxed = boxed[:pair_count].reshape(epochs_here, 2 * SLOTS, look_rows, col_count)
    power_box = boxed[pair_count:]
    coh_real = pair_boxed[:, 0::2]
    coh_imag = pair_boxed[:, 1::2]
    denominator = power_box[:epochs_here, None] * jnp.take(power_box, partner, axis=0) + EPSILON
    coherence = (coh_real * coh_real + coh_imag * coh_imag) / denominator
    observed = coh_imag / jnp.sqrt(denominator)
    est_ahead = passed_along(estimate, "epoch", -1)
    est_extended = jnp.concatenate([estimate, est_ahead], axis=0)
    fitted = estimate[:, None] - jnp.take(est_extended, partner, axis=0)
    factor = weights[:, :, None, None] * coherence
    weighted = factor * (observed - fitted)
    flattened = weighted.reshape(epochs_here * SLOTS, look_rows * col_count)
    selector = (
        jnp.arange(epochs_here + OFFS, dtype=jnp.int32)[:, None] == partner.reshape(1, -1)
    ).astype(jnp.float32)
    gathered = jnp.dot(
        selector, flattened, precision=lax.Precision.HIGHEST, preferred_element_type=jnp.float32
    ).reshape(epochs_here + OFFS, look_rows, col_count)
    own_part = jnp.sum(weighted, axis=1) - gathered[:epochs_here]
    returned = passed_along(-gathered[epochs_here:], "epoch", 1)
    gradient = jnp.concatenate([own_part + returned, own_part[OFFS:]], axis=0)
    cell_count = float(
        epochs_here
        * lax.axis_size("epoch")
        * look_rows
        * lax.axis_size("space")
        * col_count
        * lax.axis_size("sub")
    )
    local_norm = jnp.sum(gradient * gradient)
    local_crossed = jnp.sum(gradient * direction)
    mean_before = prev_mean[0]
    fields_ahead = passed_along(
        jnp.stack([gradient, direction]).astype(jnp.bfloat16), "epoch", -1
    ).astype(jnp.float32)
    grad_extended = jnp.concatenate([gradient, fields_ahead[0]], axis=0)
    old_extended = jnp.concatenate([direction, fields_ahead[1]], axis=0)
    grad_spread = gradient[:, None] - jnp.take(grad_extended, partner, axis=0)
    old_spread = direction[:, None] - jnp.take(old_extended, partner, axis=0)
    totals = lax.psum(
        (
            local_norm,
            local_crossed,
            jnp.sum(factor * grad_spread * grad_spread),
            jnp.sum(factor * grad_spread * old_spread),
            jnp.sum(factor * old_spread * old_spread),
        ),
        ("epoch", "space", "sub"),
    )
    grad_norm, crossed, grad_term, mixed_term, old_term = totals
    momentum = grad_norm / cell_count / mean_before
    new_direction = gradient + momentum * direction
    curvature = grad_term + 2.0 * momentum * mixed_term + momentum * momentum * old_term
    along_sum = grad_norm + momentum * crossed
    step_size = along_sum / curvature
    return (estimate + step_size * new_direction, new_direction)


def solution(mesh):
    return jax.shard_map(
        on_device,
        mesh=mesh,
        in_specs=(
            P(None, ("groups", "epoch"), "space", "sub"),
            P(("groups", "epoch"), None),
            P(("groups", "epoch"), None),
            P(("groups", "epoch"), "space", "sub"),
            P(("groups", "epoch"), "space", "sub"),
            P(),
        ),
        out_specs=(P(("groups", "epoch"), "space", "sub"), P(("groups", "epoch"), "space", "sub")),
        check_vma=False,
    )
```

profile of v0, /device:TPU:0, one launch (start us, length us, event | category | flops | bytes accessed | tf_op | source)
XLA Modules:
  0.0 223.2 jit_solution(3602358008610256752)
XLA Ops:
  0.6 5.1 %collective-permute-start = (bf16[2,8,64,512]{3,2,1,0:T(8,128)(2,1)}, bf16[2,8,64,512]{3,2,1,0:T(8,128)(2,1)S(1)}, u32[]{:S(2)}, u32[]{:S(2)}) collective-permute-start(bf16[2,8,64,512]{3,2,1,0:T(8,128)(2,1)} %param.10), channel_id=1, source_target_pairs={{0,12},{4,0},{8,4},{12,8},{1,13},{5,1},{9,5},{13,9},{2,14},{6,2},{... | collective-permute-start | bytes 3145736 | tf_op jit(solution)/shard_map/ppermute | solution.py:15
  7.8 20.7 %collective-permute-done = bf16[2,8,64,512]{3,2,1,0:T(8,128)(2,1)S(1)} collective-permute-done((bf16[2,8,64,512]{3,2,1,0:T(8,128)(2,1)}, bf16[2,8,64,512]{3,2,1,0:T(8,128)(2,1)S(1)}, u32[]{:S(2)}, u32[]{:S(2)}) %collective-permute-start) | collective-permute-done | bytes 1048608 | tf_op jit(solution)/shard_map/ppermute | solution.py:15
  32.2 3.2 %gather_fusion.5 = f32[8,64,512]{2,1,0:T(8,128)} fusion(f32[16,64,512]{2,1,0:T(8,128)} %get-tuple-element.42, s32[1024]{0:T(1024)S(1)} %get-tuple-element.61), kind=kCustom, calls=%fused_computation.6.clone | custom fusion | bytes 2097184 | tf_op jit(solution)/shard_map/jit(_take)/gather | solution.py:60
  37.0 3.3 %gather_fusion.1 = f32[8,64,512]{2,1,0:T(8,128)} fusion(f32[16,64,512]{2,1,0:T(8,128)} %get-tuple-element.42, s32[1024]{0:T(1024)S(1)} %get-tuple-element.63), kind=kCustom, calls=%fused_computation.2.clone | custom fusion | bytes 2097184 | tf_op jit(solution)/shard_map/jit(_take)/gather | solution.py:60
  41.8 3.2 %gather_fusion.7 = f32[8,64,512]{2,1,0:T(8,128)} fusion(f32[16,64,512]{2,1,0:T(8,128)} %get-tuple-element.42, s32[1024]{0:T(1024)S(1)} %get-tuple-element.60), kind=kCustom, calls=%fused_computation.8.clone | custom fusion | bytes 2097184 | tf_op jit(solution)/shard_map/jit(_take)/gather | solution.py:60
  46.7 3.2 %gather_fusion.3 = f32[8,64,512]{2,1,0:T(8,128)} fusion(f32[16,64,512]{2,1,0:T(8,128)} %get-tuple-element.42, s32[1024]{0:T(1024)S(1)} %get-tuple-element.62), kind=kCustom, calls=%fused_computation.4.clone | custom fusion | bytes 2097184 | tf_op jit(solution)/shard_map/jit(_take)/gather | solution.py:60
  53.4 4.8 %fusion.7 = (f32[8,64,512]{2,1,0:T(8,128)}, f32[8,64,512]{2,1,0:T(8,128)}, f32[8,64,512]{2,1,0:T(8,128)}, f32[8,64,512]{2,1,0:T(8,128)}) fusion(f32[8,64,512]{2,1,0:T(8,128)} %gather_fusion.5, f32[8,64,512]{2,1,0:T(8,128)} %gather_fusion.4, pred[8]{0:T(512)(128)(4,1)S(1)} %get-tuple-element.52, bf16[2,8,64,512]{3,2,1,0:T(8,128)(2,1)S(1)} %copy-done.1, ...), kind=kLoop, calls=%fused_computation.53 | loop fusion | flops 4718592 | bytes 9437200 | tf_op jit(solution)/shard_map/sub | solution.py:62
  69.2 4.8 %fusion.9 = (f32[8,64,512]{2,1,0:T(8,128)}, f32[8,64,512]{2,1,0:T(8,128)}, f32[8,64,512]{2,1,0:T(8,128)}, f32[8,64,512]{2,1,0:T(8,128)}) fusion(f32[8,64,512]{2,1,0:T(8,128)} %gather_fusion.7, f32[8,64,512]{2,1,0:T(8,128)} %gather_fusion.6, pred[8]{0:T(512)(128)(4,1)S(1)} %get-tuple-element.21, bf16[2,8,64,512]{3,2,1,0:T(8,128)(2,1)S(1)} %copy-done.1, ...), kind=kLoop, calls=%fused_computation.55 | loop fusion | flops 4718592 | bytes 9437200 | tf_op jit(solution)/shard_map/sub | solution.py:62
  74.0 2.6 %reshape.76 = f32[8,16,4,512]{3,2,1,0:T(4,128)} reshape(f32[8,64,512]{2,1,0:T(8,128)} %get-tuple-element.43) | data formatting | bytes 2097152 | tf_op jit(solution)/shard_map/reshape | solution.py:33
  76.6 2.6 %reduce_sum.137 = f32[8,16,512]{2,1,0:T(8,128)} reduce(f32[8,16,4,512]{3,2,1,0:T(4,128)} %reshape.76, f32[]{:T(128)} %constant.20.clone.1), dimensions={2}, to_apply=%region_2.4 | reduce | flops 196608 | bytes 1310724 | tf_op jit(solution)/shard_map/reduce_sum | solution.py:33
  80.5 2.7 %reduce_sum.138 = f32[8,16,512]{2,1,0:T(8,128)} reduce(f32[8,16,4,512]{3,2,1,0:T(4,128)} %reshape.77, f32[]{:T(128)} %constant.20.clone.1), dimensions={2}, to_apply=%region_3.5 | reduce | flops 196608 | bytes 1310724 | tf_op jit(solution)/shard_map/reduce_sum | solution.py:33
  85.7 2.6 %reduce_sum.139 = f32[8,16,512]{2,1,0:T(8,128)} reduce(f32[8,16,4,512]{3,2,1,0:T(4,128)} %reshape.78, f32[]{:T(128)} %constant.20.clone.1), dimensions={2}, to_apply=%region_4.6 | reduce | flops 196608 | bytes 1310724 | tf_op jit(solution)/shard_map/reduce_sum | solution.py:33
  89.5 2.7 %reduce_sum.140 = f32[8,16,512]{2,1,0:T(8,128)} reduce(f32[8,16,4,512]{3,2,1,0:T(4,128)} %reshape.79, f32[]{:T(128)} %constant.20.clone.1), dimensions={2}, to_apply=%region_5.7 | reduce | flops 196608 | bytes 1310724 | tf_op jit(solution)/shard_map/reduce_sum | solution.py:33
  98.5 2.6 %reduce_sum.142 = f32[8,16,512]{2,1,0:T(8,128)} reduce(f32[8,16,4,512]{3,2,1,0:T(4,128)} %reshape.81, f32[]{:T(128)} %constant.20.clone.1), dimensions={2}, to_apply=%region_7.9 | reduce | flops 196608 | bytes 1310724 | tf_op jit(solution)/shard_map/reduce_sum | solution.py:33
  105.5 5.9 %collective-permute-start.1 = (f32[80,3,512]{2,0,1:T(8,128)}, f32[80,3,512]{2,0,1:T(8,128)}, u32[]{:S(2)}, u32[]{:S(2)}) collective-permute-start(f32[80,3,512]{2,0,1:T(8,128)} %copy.55), channel_id=1, source_target_pairs={{0,2},{1,3},{4,6},{5,7},{8,10},{9,11},{12,14},{13,15},{16,18},{17,... | collective-permute-start | bytes 1474568 | tf_op jit(solution)/shard_map/ppermute | solution.py:23
  111.4 4.2 %collective-permute-start.5 = (f32[8,16,512]{2,1,0:T(8,128)S(1)}, f32[8,16,512]{2,1,0:T(8,128)}, u32[]{:S(2)}, u32[]{:S(2)}) collective-permute-start(f32[8,16,512]{2,1,0:T(8,128)S(1)} %copy-done.8), channel_id=1, source_target_pairs={{0,12},{4,0},{8,4},{12,8},{1,13},{5,1},{9,5},{13,9},{2,14},{6,2},{... | collective-permute-start | bytes 786440 | tf_op jit(solution)/shard_map/ppermute | solution.py:15
  129.1 4.2 %collective-permute-start.3 = (f32[80,22,3]{0,1,2:T(8,128)}, f32[80,22,3]{0,1,2:T(8,128)}, u32[]{:S(2)}, u32[]{:S(2)}) collective-permute-start(f32[80,22,3]{0,1,2:T(8,128)} %copy.59), channel_id=1, source_target_pairs={{0,1},{2,3},{4,5},{6,7},{8,9},{10,11},{12,13},{14,15},{16,17},{18,... | collective-permute-start | bytes 63368 | tf_op jit(solution)/shard_map/ppermute | solution.py:23
  135.1 2.7 %gather_fusion.9 = f32[32,16,512]{2,1,0:T(8,128)} fusion(f32[16,16,512]{2,1,0:T(8,128)} %pad_maximum_fusion.7, s32[1024]{0:T(1024)S(1)} %pad_clamp_fusion), kind=kCustom, calls=%fused_computation.9.clone | custom fusion | bytes 2097280 | tf_op jit(solution)/shard_map/jit(_take)/gather | solution.py:78
  142.0 6.8 %pad_maximum_fusion = f32[80,22,518]{2,1,0:T(8,128)S(1)} fusion(f32[80,22,3]{2,1,0:T(8,128)} %copy.62, f32[80,3,512]{2,1,0:T(4,128)S(1)} %copy.58, f32[16,16,512]{2,1,0:T(8,128)S(1)} %copy-done.2, f32[64,16,512]{2,1,0:T(8,128)S(1)} %bitcast.80, f32[80,3,512]{2,1,0:T(4,128)} %copy-done.3, f32[80,22,3]{2,1,0:T(8,128)} %copy.61), kind=kLoop, calls=%fused_computation.12 | loop fusion | flops 4558400 | bytes 7293440 | tf_op jit(solution)/shard_map/concatenate | solution.py:27
  150.8 4.2 %slice_add_fusion.6 = f32[80,16,512]{2,1,0:T(8,128)S(1)} fusion(f32[80,16,518]{2,1,0:T(8,128)S(1)} %slice_add_fusion), kind=kLoop, calls=%fused_computation.39 | loop fusion | flops 3932160 | bytes 20971520 | tf_op jit(solution)/shard_map/add | solution.py:40
  158.9 2.8 %fusion.17 = (f32[8,16,512]{2,1,0:T(8,128)S(1)}, f32[8,4,16,512]{3,2,1,0:T(8,128)S(1)}, f32[8,4,16,512]{3,2,1,0:T(8,128)S(1)}) fusion(f32[8,16,512]{2,1,0:T(8,128)S(1)} %copy-done.8, pred[8,4]{1,0:T(8,128)(4,1)S(1)} %copy.63, f32[8,16,512]{2,1,0:T(8,128)S(1)} %slice-done, f32[8,8,16,512]{3,2,1,0:T(8,128)} %bitcast.81, f32[8,4]{1,0:T(8,128)S(1)} %copy.54, ...), kind=kLoop, calls=%fused_computation.116 | loop fusion | flops 3604480 | bytes 7078048 | tf_op jit(solution)/shard_map/reduce_sum | solution.py:88
  163.4 9.1 %collective-permute-done.6 = f32[8,16,512]{2,1,0:T(8,128)S(1)} collective-permute-done((f32[8,16,512]{2,1,0:T(8,128)S(1)}, f32[8,16,512]{2,1,0:T(8,128)S(1)}, u32[]{:S(2)}, u32[]{:S(2)}) %collective-permute-start.6) | collective-permute-done | bytes 262176 | tf_op jit(solution)/shard_map/ppermute | solution.py:15
  175.9 4.0 %collective-permute-done.7 = bf16[2,8,16,512]{3,2,1,0:T(8,128)(2,1)S(1)} collective-permute-done((bf16[2,8,16,512]{3,2,1,0:T(8,128)(2,1)S(1)}, bf16[2,8,16,512]{3,2,1,0:T(8,128)(2,1)S(1)}, u32[]{:S(2)}, u32[]{:S(2)}) %collective-permute-start.7) | collective-permute-done | bytes 262176 | tf_op jit(solution)/shard_map/ppermute | solution.py:15
  186.4 32.0 %all-reduce = (f32[]{:T(128)}, f32[]{:T(128)}, f32[]{:T(128)}, f32[]{:T(128)}, f32[]{:T(128)}) all-reduce(f32[]{:T(128)} %get-tuple-element.8, f32[]{:T(128)} %get-tuple-element.7, f32[]{:T(128)} %get-tuple-element.6, f32[]{:T(128)} %get-tuple-element.5, ...), channel_id=1, replica_groups=mesh['groups'=2,'epoch'=4,'space'=2,'sub'=2] {'epoch','space','sub'}, use_global_device_ids=true, to_apply=%region_11.14 | all-reduce | flops 5 | bytes 40 | tf_op jit(solution)/shard_map/psum | solution.py:109
  (113 shorter events, 77.6 us)
Async XLA Ops:
  0.6 27.9 %collective-permute-start = (bf16[2,8,64,512]{3,2,1,0:T(8,128)(2,1)}, bf16[2,8,64,512]{3,2,1,0:T(8,128)(2,1)S(1)}, u32[]{:S(2)}, u32[]{:S(2)}) collective-permute-start(bf16[2,8,64,512]{3,2,1,0:T(8,128)(2,1)} %param.10), channel_id=1, source_target_pairs={{0,12},{4,0},{8,4},{12,8},{1,13},{5,1},{9,5},{13,9},{2,14},{6,2},{... | collective-permute-start | bytes 3145736 | tf_op jit(solution)/shard_map/ppermute | solution.py:15
  51.4 2.0 copy-start.1
  74.0 5.2 %copy-start.6 = (f32[8,64,512]{2,1,0:T(8,128)S(1)}, f32[8,64,512]{2,1,0:T(8,128)}, u32[]{:S(2)}) copy-start(f32[8,64,512]{2,1,0:T(8,128)} %get-tuple-element.44) | copy-start | bytes 3145732
  80.5 7.7 %copy-start.4 = (f32[8,64,512]{2,1,0:T(8,128)S(1)}, f32[8,64,512]{2,1,0:T(8,128)}, u32[]{:S(2)}) copy-start(f32[8,64,512]{2,1,0:T(8,128)} %get-tuple-element.33) | copy-start | bytes 3145732
  89.5 7.7 %copy-start.5 = (f32[8,64,512]{2,1,0:T(8,128)S(1)}, f32[8,64,512]{2,1,0:T(8,128)}, u32[]{:S(2)}) copy-start(f32[8,64,512]{2,1,0:T(8,128)} %get-tuple-element.31) | copy-start | bytes 3145732
  98.5 3.8 %copy-start.9 = (f32[8,16,512]{2,1,0:T(8,128)S(1)}, f32[8,16,512]{2,1,0:T(8,128)}, u32[]{:S(2)}) copy-start(f32[8,16,512]{2,1,0:T(8,128)} %reduce_sum.138) | copy-start | bytes 786436
  98.5 3.8 %copy-start.10 = (f32[8,16,512]{2,1,0:T(8,128)S(1)}, f32[8,16,512]{2,1,0:T(8,128)}, u32[]{:S(2)}) copy-start(f32[8,16,512]{2,1,0:T(8,128)} %reduce_sum.139) | copy-start | bytes 786436
  101.2 1.2 copy-start.12
  101.2 1.3 copy-start.13
  101.2 1.4 copy-start.2
  102.9 8.6 %copy-start.8 = (f32[8,16,512]{2,1,0:T(8,128)S(1)}, f32[8,16,512]{2,1,0:T(8,128)}, u32[]{:S(2)}) copy-start(f32[8,16,512]{2,1,0:T(8,128)} %param.13) | copy-start | bytes 786436
  102.9 12.8 %copy-start.14 = (s32[8,4]{0,1:T(4,128)S(1)}, s32[8,4]{0,1:T(4,128)}, u32[]{:S(2)}) copy-start(s32[8,4]{0,1:T(4,128)} %param.11) | copy-start | bytes 388
  102.9 12.9 %copy-start.15 = (f32[8,4]{0,1:T(4,128)S(1)}, f32[8,4]{0,1:T(4,128)}, u32[]{:S(2)}) copy-start(f32[8,4]{0,1:T(4,128)} %param.12) | copy-start | bytes 388
  103.1 14.1 %collective-permute-start.2 = (f32[80,3,512]{2,0,1:T(8,128)S(1)}, f32[80,3,512]{2,0,1:T(8,128)}, u32[]{:S(2)}, u32[]{:S(2)}) collective-permute-start(f32[80,3,512]{2,0,1:T(8,128)S(1)} %copy.56), channel_id=1, source_target_pairs={{2,0},{3,1},{6,4},{7,5},{10,8},{11,9},{14,12},{15,13},{18,16},{19,... | collective-permute-start | bytes 1474568 | tf_op jit(solution)/shard_map/ppermute | solution.py:26
  105.5 14.8 %collective-permute-start.1 = (f32[80,3,512]{2,0,1:T(8,128)}, f32[80,3,512]{2,0,1:T(8,128)}, u32[]{:S(2)}, u32[]{:S(2)}) collective-permute-start(f32[80,3,512]{2,0,1:T(8,128)} %copy.55), channel_id=1, source_target_pairs={{0,2},{1,3},{4,6},{5,7},{8,10},{9,11},{12,14},{13,15},{16,18},{17,... | collective-permute-start | bytes 1474568 | tf_op jit(solution)/shard_map/ppermute | solution.py:23
  111.4 21.9 %collective-permute-start.5 = (f32[8,16,512]{2,1,0:T(8,128)S(1)}, f32[8,16,512]{2,1,0:T(8,128)}, u32[]{:S(2)}, u32[]{:S(2)}) collective-permute-start(f32[8,16,512]{2,1,0:T(8,128)S(1)} %copy-done.8), channel_id=1, source_target_pairs={{0,12},{4,0},{8,4},{12,8},{1,13},{5,1},{9,5},{13,9},{2,14},{6,2},{... | collective-permute-start | bytes 786440 | tf_op jit(solution)/shard_map/ppermute | solution.py:15
  121.6 1.9 copy-start.3
  125.7 12.2 %collective-permute-start.4 = (f32[80,22,3]{0,1,2:T(8,128)}, f32[80,22,3]{0,1,2:T(8,128)}, u32[]{:S(2)}, u32[]{:S(2)}) collective-permute-start(f32[80,22,3]{0,1,2:T(8,128)} %copy.60), channel_id=1, source_target_pairs={{1,0},{3,2},{5,4},{7,6},{9,8},{11,10},{13,12},{15,14},{17,16},{19,... | collective-permute-start | bytes 63368 | tf_op jit(solution)/shard_map/ppermute | solution.py:26
  129.1 10.8 %collective-permute-start.3 = (f32[80,22,3]{0,1,2:T(8,128)}, f32[80,22,3]{0,1,2:T(8,128)}, u32[]{:S(2)}, u32[]{:S(2)}) collective-permute-start(f32[80,22,3]{0,1,2:T(8,128)} %copy.59), channel_id=1, source_target_pairs={{0,1},{2,3},{4,5},{6,7},{8,9},{10,11},{12,13},{14,15},{16,17},{18,... | collective-permute-start | bytes 63368 | tf_op jit(solution)/shard_map/ppermute | solution.py:23
  155.0 2.2 copy-start
  157.2 1.6 slice-start
  162.3 10.4 %copy-start.7 = (f32[8,16,512]{2,1,0:T(8,128)S(1)}, f32[8,16,512]{2,1,0:T(8,128)}, u32[]{:S(2)}) copy-start(f32[8,16,512]{2,1,0:T(8,128)} %param.14) | copy-start | bytes 786436
  163.0 9.5 %collective-permute-start.6 = (f32[8,16,512]{2,1,0:T(8,128)S(1)}, f32[8,16,512]{2,1,0:T(8,128)S(1)}, u32[]{:S(2)}, u32[]{:S(2)}) collective-permute-start(f32[8,16,512]{2,1,0:T(8,128)S(1)} %copy.69), channel_id=1, source_target_pairs={{0,4},{4,8},{8,12},{12,0},{1,5},{5,9},{9,13},{13,1},{2,6},{6,10},{... | collective-permute-start | bytes 786440 | tf_op jit(solution)/shard_map/ppermute | solution.py:15
  173.5 6.4 %collective-permute-start.7 = (bf16[2,8,16,512]{3,2,1,0:T(8,128)(2,1)S(1)}, bf16[2,8,16,512]{3,2,1,0:T(8,128)(2,1)S(1)}, u32[]{:S(2)}, u32[]{:S(2)}) collective-permute-start(bf16[2,8,16,512]{3,2,1,0:T(8,128)(2,1)S(1)} %pad_maximum_fusion.10), channel_id=1, source_target_pairs={{0,12},{4,0},{8,4},{12,8},{1,13},{5,1},{9,5},{13,9},{2,14},{6,2},{... | collective-permute-start | bytes 786440 | tf_op jit(solution)/shard_map/ppermute | solution.py:15
  (1 other events, 1.2 us)
where the time goes:
time: 225 us; the launch traced here: 223 us
  local copies, waits for them, and re-layouts  63.5 us (28%)
  other arithmetic  60.6 us (27%)
  waiting for transfers between devices  36.6 us (16%)
  blocking collectives  32 us (14%)
  starting transfers between devices  24.4 us (11%)
  between operations  5.64 us (3%)
    ppermute x4, waiting for transfers between devices, passed_along(): return lax.ppermute(x, axis, [(i, (i + by) % size) for i in range(size)])  33.8 us
    psum x1, blocking collectives, on_device(): lax.psum((local_norm, local_crossed, jnp.sum(factor * grad_spread * grad_...  32 us
    reduce_sum x9, other arithmetic, looked_sum(): jnp.sum(field.reshape(shape[:-2] + (shape[-2] // LOOK, LOOK, shape[-1])),...  21.5 us
    reshape x8, local copies, waits for them, and re-layouts, looked_sum(): field.reshape(shape[:-2] + (shape[-2] // LOOK, LOOK, shape[-1]))  16.5 us
    gather x4, local copies, waits for them, and re-layouts, on_device(): mate_imag = jnp.take(ext_imag, partner[:, slot_index], axis=0)  12.8 us
    ppermute x4, starting transfers between devices, passed_along(): return lax.ppermute(x, axis, [(i, (i + by) % size) for i in range(size)])  11.5 us
    ppermute x2, starting transfers between devices, extended_2(): lax.ppermute(lax.slice_in_dim(block, block.shape[dim] - width, None, axis...  10.2 us
    sub x2, other arithmetic, on_device(): pieces.append(looked_sum(own_imag * mate_real - own_real * mate_imag))  9.68 us
  transfers between devices with their start and end apart: 8, of which 5 were waited for; matrix products, arithmetic and copies ran while one was open for 8% of the time, Pallas kernels for 0%

commit v1 on v0

--- a/solution.py
+++ b/solution.py
@@ -8,6 +8,9 @@
 LOOK = 4
 RADIUS = 3
 EPSILON = 1e-06
+area_report = lambda row_data, axis_name, group_axis: jax.lax.psum(
+    jax.lax.psum(row_data, axis_name), group_axis
+)
 
 
 def passed_along(x, axis, by):
@@ -106,7 +109,7 @@
     old_extended = jnp.concatenate([direction, fields_ahead[1]], axis=0)
     grad_spread = gradient[:, None] - jnp.take(grad_extended, partner, axis=0)
     old_spread = direction[:, None] - jnp.take(old_extended, partner, axis=0)
-    totals = lax.psum(
+    totals = area_report(
         (
             local_norm,
             local_crossed,
@@ -114,7 +117,8 @@
             jnp.sum(factor * grad_spread * old_spread),
             jnp.sum(factor * old_spread * old_spread),
         ),
-        ("epoch", "space", "sub"),
+        "epoch",
+        ("space", "sub"),
     )
     grad_norm, crossed, grad_term, mixed_term, old_term = totals
     momentum = grad_norm / cell_count / mean_before

time: 225 us -> 212 us (0.942)
  blocking collectives: 32 us -> 19.2 us
    psum x1 -> x2, blocking collectives: 32 us -> 19.2 us  [the longest x1 12.5 us: jax.lax.psum(row_data, axis_name)]
  transfers between devices with their start and end apart: 8 -> 8, of which waited for: 5 -> 5; matrix products, arithmetic and copies ran while one was open for 8% -> 9% of each run, Pallas kernels for 0% -> 0%
where the time goes in v1:
time: 212 us; the launch traced here: 210 us
  local copies, waits for them, and re-layouts  63.5 us (30%)
  other arithmetic  60.6 us (29%)
  waiting for transfers between devices  36.6 us (17%)
  starting transfers between devices  24.4 us (12%)
  blocking collectives  19.2 us (9%)
  between operations  5.56 us (3%)
    ppermute x4, waiting for transfers between devices, passed_along(): return lax.ppermute(x, axis, [(i, (i + by) % size) for i in range(size)])  33.8 us
    reduce_sum x9, other arithmetic, looked_sum(): jnp.sum(field.reshape(shape[:-2] + (shape[-2] // LOOK, LOOK, shape[-1])),...  21.5 us
    reshape x8, local copies, waits for them, and re-layouts, looked_sum(): field.reshape(shape[:-2] + (shape[-2] // LOOK, LOOK, shape[-1]))  16.5 us
    gather x4, local copies, waits for them, and re-layouts, on_device(): mate_imag = jnp.take(ext_imag, partner[:, slot_index], axis=0)  12.8 us
    psum x1, blocking collectives, jax.lax.psum(row_data, axis_name)  12.5 us
    ppermute x4, starting transfers between devices, passed_along(): return lax.ppermute(x, axis, [(i, (i + by) % size) for i in range(size)])  11.5 us
    ppermute x2, starting transfers between devices, extended_2(): lax.ppermute(lax.slice_in_dim(block, block.shape[dim] - width, None, axis...  10.2 us
    sub x2, other arithmetic, on_device(): pieces.append(looked_sum(own_imag * mate_real - own_real * mate_imag))  9.68 us
  transfers between devices with their start and end apart: 8, of which 5 were waited for; matrix products, arithmetic and copies ran while one was open for 9% of the time, Pallas kernels for 0%

profile of v1, /device:TPU:0, one launch (start us, length us, event | category | flops | bytes accessed | tf_op | source)
XLA Modules:
  0.0 210.4 jit_solution(14228615158309159108)
XLA Ops:
  0.6 5.1 %collective-permute-start = (bf16[2,8,64,512]{3,2,1,0:T(8,128)(2,1)}, bf16[2,8,64,512]{3,2,1,0:T(8,128)(2,1)S(1)}, u32[]{:S(2)}, u32[]{:S(2)}) collective-permute-start(bf16[2,8,64,512]{3,2,1,0:T(8,128)(2,1)} %param.10), channel_id=1, source_target_pairs={{0,12},{4,0},{8,4},{12,8},{1,13},{5,1},{9,5},{13,9},{2,14},{6,2},{... | collective-permute-start | bytes 3145736 | tf_op jit(solution)/shard_map/ppermute | solution.py:18
  7.8 20.7 %collective-permute-done = bf16[2,8,64,512]{3,2,1,0:T(8,128)(2,1)S(1)} collective-permute-done((bf16[2,8,64,512]{3,2,1,0:T(8,128)(2,1)}, bf16[2,8,64,512]{3,2,1,0:T(8,128)(2,1)S(1)}, u32[]{:S(2)}, u32[]{:S(2)}) %collective-permute-start) | collective-permute-done | bytes 1048608 | tf_op jit(solution)/shard_map/ppermute | solution.py:18
  32.2 3.2 %gather_fusion.5 = f32[8,64,512]{2,1,0:T(8,128)} fusion(f32[16,64,512]{2,1,0:T(8,128)} %get-tuple-element.47, s32[1024]{0:T(1024)S(1)} %get-tuple-element.66), kind=kCustom, calls=%fused_computation.6.clone | custom fusion | bytes 2097184 | tf_op jit(solution)/shard_map/jit(_take)/gather | solution.py:63
  37.0 3.3 %gather_fusion.1 = f32[8,64,512]{2,1,0:T(8,128)} fusion(f32[16,64,512]{2,1,0:T(8,128)} %get-tuple-element.47, s32[1024]{0:T(1024)S(1)} %get-tuple-element.68), kind=kCustom, calls=%fused_computation.2.clone | custom fusion | bytes 2097184 | tf_op jit(solution)/shard_map/jit(_take)/gather | solution.py:63
  41.8 3.2 %gather_fusion.7 = f32[8,64,512]{2,1,0:T(8,128)} fusion(f32[16,64,512]{2,1,0:T(8,128)} %get-tuple-element.47, s32[1024]{0:T(1024)S(1)} %get-tuple-element.65), kind=kCustom, calls=%fused_computation.8.clone | custom fusion | bytes 2097184 | tf_op jit(solution)/shard_map/jit(_take)/gather | solution.py:63
  46.7 3.2 %gather_fusion.3 = f32[8,64,512]{2,1,0:T(8,128)} fusion(f32[16,64,512]{2,1,0:T(8,128)} %get-tuple-element.47, s32[1024]{0:T(1024)S(1)} %get-tuple-element.67), kind=kCustom, calls=%fused_computation.4.clone | custom fusion | bytes 2097184 | tf_op jit(solution)/shard_map/jit(_take)/gather | solution.py:63
  53.4 4.8 %fusion.7 = (f32[8,64,512]{2,1,0:T(8,128)}, f32[8,64,512]{2,1,0:T(8,128)}, f32[8,64,512]{2,1,0:T(8,128)}, f32[8,64,512]{2,1,0:T(8,128)}) fusion(f32[8,64,512]{2,1,0:T(8,128)} %gather_fusion.5, f32[8,64,512]{2,1,0:T(8,128)} %gather_fusion.4, pred[8]{0:T(512)(128)(4,1)S(1)} %get-tuple-element.57, bf16[2,8,64,512]{3,2,1,0:T(8,128)(2,1)S(1)} %copy-done.1, ...), kind=kLoop, calls=%fused_computation.53 | loop fusion | flops 4718592 | bytes 9437200 | tf_op jit(solution)/shard_map/sub | solution.py:65
  69.2 4.8 %fusion.9 = (f32[8,64,512]{2,1,0:T(8,128)}, f32[8,64,512]{2,1,0:T(8,128)}, f32[8,64,512]{2,1,0:T(8,128)}, f32[8,64,512]{2,1,0:T(8,128)}) fusion(f32[8,64,512]{2,1,0:T(8,128)} %gather_fusion.7, f32[8,64,512]{2,1,0:T(8,128)} %gather_fusion.6, pred[8]{0:T(512)(128)(4,1)S(1)} %get-tuple-element.26, bf16[2,8,64,512]{3,2,1,0:T(8,128)(2,1)S(1)} %copy-done.1, ...), kind=kLoop, calls=%fused_computation.55 | loop fusion | flops 4718592 | bytes 9437200 | tf_op jit(solution)/shard_map/sub | solution.py:65
  74.0 2.6 %reshape.76 = f32[8,16,4,512]{3,2,1,0:T(4,128)} reshape(f32[8,64,512]{2,1,0:T(8,128)} %get-tuple-element.48) | data formatting | bytes 2097152 | tf_op jit(solution)/shard_map/reshape | solution.py:36
  76.6 2.6 %reduce_sum.137 = f32[8,16,512]{2,1,0:T(8,128)} reduce(f32[8,16,4,512]{3,2,1,0:T(4,128)} %reshape.76, f32[]{:T(128)} %constant.20.clone.1), dimensions={2}, to_apply=%region_2.4 | reduce | flops 196608 | bytes 1310724 | tf_op jit(solution)/shard_map/reduce_sum | solution.py:36
  80.5 2.7 %reduce_sum.138 = f32[8,16,512]{2,1,0:T(8,128)} reduce(f32[8,16,4,512]{3,2,1,0:T(4,128)} %reshape.77, f32[]{:T(128)} %constant.20.clone.1), dimensions={2}, to_apply=%region_3.5 | reduce | flops 196608 | bytes 1310724 | tf_op jit(solution)/shard_map/reduce_sum | solution.py:36
  89.5 2.7 %reduce_sum.140 = f32[8,16,512]{2,1,0:T(8,128)} reduce(f32[8,16,4,512]{3,2,1,0:T(4,128)} %reshape.79, f32[]{:T(128)} %constant.20.clone.1), dimensions={2}, to_apply=%region_5.7 | reduce | flops 196608 | bytes 1310724 | tf_op jit(solution)/shard_map/reduce_sum | solution.py:36
  98.5 2.6 %reduce_sum.142 = f32[8,16,512]{2,1,0:T(8,128)} reduce(f32[8,16,4,512]{3,2,1,0:T(4,128)} %reshape.81, f32[]{:T(128)} %constant.20.clone.1), dimensions={2}, to_apply=%region_7.9 | reduce | flops 196608 | bytes 1310724 | tf_op jit(solution)/shard_map/reduce_sum | solution.py:36
  105.5 5.9 %collective-permute-start.1 = (f32[80,3,512]{2,0,1:T(8,128)}, f32[80,3,512]{2,0,1:T(8,128)}, u32[]{:S(2)}, u32[]{:S(2)}) collective-permute-start(f32[80,3,512]{2,0,1:T(8,128)} %copy.55), channel_id=1, source_target_pairs={{0,2},{1,3},{4,6},{5,7},{8,10},{9,11},{12,14},{13,15},{16,18},{17,... | collective-permute-start | bytes 1474568 | tf_op jit(solution)/shard_map/ppermute | solution.py:26
  111.4 4.2 %collective-permute-start.5 = (f32[8,16,512]{2,1,0:T(8,128)S(1)}, f32[8,16,512]{2,1,0:T(8,128)}, u32[]{:S(2)}, u32[]{:S(2)}) collective-permute-start(f32[8,16,512]{2,1,0:T(8,128)S(1)} %copy-done.8), channel_id=1, source_target_pairs={{0,12},{4,0},{8,4},{12,8},{1,13},{5,1},{9,5},{13,9},{2,14},{6,2},{... | collective-permute-start | bytes 786440 | tf_op jit(solution)/shard_map/ppermute | solution.py:18
  129.1 4.2 %collective-permute-start.3 = (f32[80,22,3]{0,1,2:T(8,128)}, f32[80,22,3]{0,1,2:T(8,128)}, u32[]{:S(2)}, u32[]{:S(2)}) collective-permute-start(f32[80,22,3]{0,1,2:T(8,128)} %copy.59), channel_id=1, source_target_pairs={{0,1},{2,3},{4,5},{6,7},{8,9},{10,11},{12,13},{14,15},{16,17},{18,... | collective-permute-start | bytes 63368 | tf_op jit(solution)/shard_map/ppermute | solution.py:26
  135.1 2.7 %gather_fusion.9 = f32[32,16,512]{2,1,0:T(8,128)} fusion(f32[16,16,512]{2,1,0:T(8,128)} %pad_maximum_fusion.7, s32[1024]{0:T(1024)S(1)} %pad_clamp_fusion), kind=kCustom, calls=%fused_computation.9.clone | custom fusion | bytes 2097280 | tf_op jit(solution)/shard_map/jit(_take)/gather | solution.py:81
  142.0 6.8 %pad_maximum_fusion = f32[80,22,518]{2,1,0:T(8,128)S(1)} fusion(f32[80,22,3]{2,1,0:T(8,128)} %copy.62, f32[80,3,512]{2,1,0:T(4,128)S(1)} %copy.58, f32[16,16,512]{2,1,0:T(8,128)S(1)} %copy-done.2, f32[64,16,512]{2,1,0:T(8,128)S(1)} %bitcast.80, f32[80,3,512]{2,1,0:T(4,128)} %copy-done.3, f32[80,22,3]{2,1,0:T(8,128)} %copy.61), kind=kLoop, calls=%fused_computation.12 | loop fusion | flops 4558400 | bytes 7293440 | tf_op jit(solution)/shard_map/concatenate | solution.py:30
  150.8 4.2 %slice_add_fusion.6 = f32[80,16,512]{2,1,0:T(8,128)S(1)} fusion(f32[80,16,518]{2,1,0:T(8,128)S(1)} %slice_add_fusion), kind=kLoop, calls=%fused_computation.39 | loop fusion | flops 3932160 | bytes 20971520 | tf_op jit(solution)/shard_map/add | solution.py:43
  158.9 2.8 %fusion.17 = (f32[8,16,512]{2,1,0:T(8,128)S(1)}, f32[8,4,16,512]{3,2,1,0:T(8,128)S(1)}, f32[8,4,16,512]{3,2,1,0:T(8,128)S(1)}) fusion(f32[8,16,512]{2,1,0:T(8,128)S(1)} %copy-done.8, pred[8,4]{1,0:T(8,128)(4,1)S(1)} %copy.63, f32[8,16,512]{2,1,0:T(8,128)S(1)} %slice-done, f32[8,8,16,512]{3,2,1,0:T(8,128)} %bitcast.81, f32[8,4]{1,0:T(8,128)S(1)} %copy.54, ...), kind=kLoop, calls=%fused_computation.116 | loop fusion | flops 3604480 | bytes 7078048 | tf_op jit(solution)/shard_map/reduce_sum | solution.py:91
  163.4 9.1 %collective-permute-done.6 = f32[8,16,512]{2,1,0:T(8,128)S(1)} collective-permute-done((f32[8,16,512]{2,1,0:T(8,128)S(1)}, f32[8,16,512]{2,1,0:T(8,128)S(1)}, u32[]{:S(2)}, u32[]{:S(2)}) %collective-permute-start.6) | collective-permute-done | bytes 262176 | tf_op jit(solution)/shard_map/ppermute | solution.py:18
  175.9 4.0 %collective-permute-done.7 = bf16[2,8,16,512]{3,2,1,0:T(8,128)(2,1)S(1)} collective-permute-done((bf16[2,8,16,512]{3,2,1,0:T(8,128)(2,1)S(1)}, bf16[2,8,16,512]{3,2,1,0:T(8,128)(2,1)S(1)}, u32[]{:S(2)}, u32[]{:S(2)}) %collective-permute-start.7) | collective-permute-done | bytes 262176 | tf_op jit(solution)/shard_map/ppermute | solution.py:18
  186.4 12.5 %all-reduce.1 = (f32[]{:T(128)}, f32[]{:T(128)}, f32[]{:T(128)}, f32[]{:T(128)}, f32[]{:T(128)}) all-reduce(f32[]{:T(128)} %get-tuple-element.8, f32[]{:T(128)} %get-tuple-element.7, f32[]{:T(128)} %get-tuple-element.6, f32[]{:T(128)} %get-tuple-element.5, ...), channel_id=1, replica_groups=mesh['groups'=2,'epoch'=4,'space'=2,'sub'=2] {'epoch'}, use_global_device_ids=true, to_apply=%region_11.14 | all-reduce | flops 5 | bytes 40 | tf_op jit(solution)/shard_map/psum | solution.py:12
  198.9 6.7 %all-reduce = (f32[]{:T(128)}, f32[]{:T(128)}, f32[]{:T(128)}, f32[]{:T(128)}, f32[]{:T(128)}) all-reduce(f32[]{:T(128)} %get-tuple-element.14, f32[]{:T(128)} %get-tuple-element.15, f32[]{:T(128)} %get-tuple-element.16, f32[]{:T(128)} %get-tuple-element.17, ...), channel_id=1, replica_groups=mesh['groups'=2,'epoch'=4,'space'=2,'sub'=2] {'space','sub'}, use_global_device_ids=true, to_apply=%region_12.15 | all-reduce | flops 5 | bytes 40 | tf_op jit(solution)/shard_map/psum | solution.py:11
  (114 shorter events, 80.2 us)
Async XLA Ops:
  0.6 27.9 %collective-permute-start = (bf16[2,8,64,512]{3,2,1,0:T(8,128)(2,1)}, bf16[2,8,64,512]{3,2,1,0:T(8,128)(2,1)S(1)}, u32[]{:S(2)}, u32[]{:S(2)}) collective-permute-start(bf16[2,8,64,512]{3,2,1,0:T(8,128)(2,1)} %param.10), channel_id=1, source_target_pairs={{0,12},{4,0},{8,4},{12,8},{1,13},{5,1},{9,5},{13,9},{2,14},{6,2},{... | collective-permute-start | bytes 3145736 | tf_op jit(solution)/shard_map/ppermute | solution.py:18
  51.4 2.0 copy-start.1
  74.0 5.2 %copy-start.6 = (f32[8,64,512]{2,1,0:T(8,128)S(1)}, f32[8,64,512]{2,1,0:T(8,128)}, u32[]{:S(2)}) copy-start(f32[8,64,512]{2,1,0:T(8,128)} %get-tuple-element.49) | copy-start | bytes 3145732
  80.5 7.7 %copy-start.4 = (f32[8,64,512]{2,1,0:T(8,128)S(1)}, f32[8,64,512]{2,1,0:T(8,128)}, u32[]{:S(2)}) copy-start(f32[8,64,512]{2,1,0:T(8,128)} %get-tuple-element.38) | copy-start | bytes 3145732
  89.5 7.7 %copy-start.5 = (f32[8,64,512]{2,1,0:T(8,128)S(1)}, f32[8,64,512]{2,1,0:T(8,128)}, u32[]{:S(2)}) copy-start(f32[8,64,512]{2,1,0:T(8,128)} %get-tuple-element.36) | copy-start | bytes 3145732
  98.5 3.8 %copy-start.9 = (f32[8,16,512]{2,1,0:T(8,128)S(1)}, f32[8,16,512]{2,1,0:T(8,128)}, u32[]{:S(2)}) copy-start(f32[8,16,512]{2,1,0:T(8,128)} %reduce_sum.138) | copy-start | bytes 786436
  98.5 3.8 %copy-start.10 = (f32[8,16,512]{2,1,0:T(8,128)S(1)}, f32[8,16,512]{2,1,0:T(8,128)}, u32[]{:S(2)}) copy-start(f32[8,16,512]{2,1,0:T(8,128)} %reduce_sum.139) | copy-start | bytes 786436
  101.2 1.2 copy-start.12
  101.2 1.3 copy-start.13
  101.2 1.4 copy-start.2
  102.9 8.6 %copy-start.8 = (f32[8,16,512]{2,1,0:T(8,128)S(1)}, f32[8,16,512]{2,1,0:T(8,128)}, u32[]{:S(2)}) copy-start(f32[8,16,512]{2,1,0:T(8,128)} %param.13) | copy-start | bytes 786436
  102.9 12.8 %copy-start.14 = (s32[8,4]{0,1:T(4,128)S(1)}, s32[8,4]{0,1:T(4,128)}, u32[]{:S(2)}) copy-start(s32[8,4]{0,1:T(4,128)} %param.11) | copy-start | bytes 388
  102.9 12.9 %copy-start.15 = (f32[8,4]{0,1:T(4,128)S(1)}, f32[8,4]{0,1:T(4,128)}, u32[]{:S(2)}) copy-start(f32[8,4]{0,1:T(4,128)} %param.12) | copy-start | bytes 388
  103.1 14.1 %collective-permute-start.2 = (f32[80,3,512]{2,0,1:T(8,128)S(1)}, f32[80,3,512]{2,0,1:T(8,128)}, u32[]{:S(2)}, u32[]{:S(2)}) collective-permute-start(f32[80,3,512]{2,0,1:T(8,128)S(1)} %copy.56), channel_id=1, source_target_pairs={{2,0},{3,1},{6,4},{7,5},{10,8},{11,9},{14,12},{15,13},{18,16},{19,... | collective-permute-start | bytes 1474568 | tf_op jit(solution)/shard_map/ppermute | solution.py:29
  105.5 14.8 %collective-permute-start.1 = (f32[80,3,512]{2,0,1:T(8,128)}, f32[80,3,512]{2,0,1:T(8,128)}, u32[]{:S(2)}, u32[]{:S(2)}) collective-permute-start(f32[80,3,512]{2,0,1:T(8,128)} %copy.55), channel_id=1, source_target_pairs={{0,2},{1,3},{4,6},{5,7},{8,10},{9,11},{12,14},{13,15},{16,18},{17,... | collective-permute-start | bytes 1474568 | tf_op jit(solution)/shard_map/ppermute | solution.py:26
  111.4 21.9 %collective-permute-start.5 = (f32[8,16,512]{2,1,0:T(8,128)S(1)}, f32[8,16,512]{2,1,0:T(8,128)}, u32[]{:S(2)}, u32[]{:S(2)}) collective-permute-start(f32[8,16,512]{2,1,0:T(8,128)S(1)} %copy-done.8), channel_id=1, source_target_pairs={{0,12},{4,0},{8,4},{12,8},{1,13},{5,1},{9,5},{13,9},{2,14},{6,2},{... | collective-permute-start | bytes 786440 | tf_op jit(solution)/shard_map/ppermute | solution.py:18
  121.6 1.9 copy-start.3
  125.7 12.2 %collective-permute-start.4 = (f32[80,22,3]{0,1,2:T(8,128)}, f32[80,22,3]{0,1,2:T(8,128)}, u32[]{:S(2)}, u32[]{:S(2)}) collective-permute-start(f32[80,22,3]{0,1,2:T(8,128)} %copy.60), channel_id=1, source_target_pairs={{1,0},{3,2},{5,4},{7,6},{9,8},{11,10},{13,12},{15,14},{17,16},{19,... | collective-permute-start | bytes 63368 | tf_op jit(solution)/shard_map/ppermute | solution.py:29
  129.1 10.8 %collective-permute-start.3 = (f32[80,22,3]{0,1,2:T(8,128)}, f32[80,22,3]{0,1,2:T(8,128)}, u32[]{:S(2)}, u32[]{:S(2)}) collective-permute-start(f32[80,22,3]{0,1,2:T(8,128)} %copy.59), channel_id=1, source_target_pairs={{0,1},{2,3},{4,5},{6,7},{8,9},{10,11},{12,13},{14,15},{16,17},{18,... | collective-permute-start | bytes 63368 | tf_op jit(solution)/shard_map/ppermute | solution.py:26
  155.0 2.2 %copy-start = (f32[80,16,512]{2,1,0:T(8,128)}, f32[80,16,512]{2,1,0:T(8,128)S(1)}, u32[]{:S(2)}) copy-start(f32[80,16,512]{2,1,0:T(8,128)S(1)} %slice_add_fusion.6) | copy-start | bytes 7864324
  157.2 1.6 slice-start
  162.3 10.4 %copy-start.7 = (f32[8,16,512]{2,1,0:T(8,128)S(1)}, f32[8,16,512]{2,1,0:T(8,128)}, u32[]{:S(2)}) copy-start(f32[8,16,512]{2,1,0:T(8,128)} %param.14) | copy-start | bytes 786436
  163.0 9.5 %collective-permute-start.6 = (f32[8,16,512]{2,1,0:T(8,128)S(1)}, f32[8,16,512]{2,1,0:T(8,128)S(1)}, u32[]{:S(2)}, u32[]{:S(2)}) collective-permute-start(f32[8,16,512]{2,1,0:T(8,128)S(1)} %copy.69), channel_id=1, source_target_pairs={{0,4},{4,8},{8,12},{12,0},{1,5},{5,9},{9,13},{13,1},{2,6},{6,10},{... | collective-permute-start | bytes 786440 | tf_op jit(solution)/shard_map/ppermute | solution.py:18
  173.5 6.4 %collective-permute-start.7 = (bf16[2,8,16,512]{3,2,1,0:T(8,128)(2,1)S(1)}, bf16[2,8,16,512]{3,2,1,0:T(8,128)(2,1)S(1)}, u32[]{:S(2)}, u32[]{:S(2)}) collective-permute-start(bf16[2,8,16,512]{3,2,1,0:T(8,128)(2,1)S(1)} %pad_maximum_fusion.10), channel_id=1, source_target_pairs={{0,12},{4,0},{8,4},{12,8},{1,13},{5,1},{9,5},{13,9},{2,14},{6,2},{... | collective-permute-start | bytes 786440 | tf_op jit(solution)/shard_map/ppermute | solution.py:18
  (1 other events, 1.2 us)
